TPU v7x, 128 devices: a whole 4x4x4 slice. The times are simulated.
128 devices in a mesh: row: 16 (over z, y_lo, core), col: 8 (over y_hi, x).
Axes of the slice: x: 4, y: 4 (y_hi: 2, y_lo: 2; y = y_hi * 2 + y_lo), z: 4, core: 2. Of those that a mesh axis runs over, the one named last changes fastest.
Arguments:
- panels: bfloat16 [1024, 32, 256], P(('row', 'col')), may hold values from -21 to 21
- tiles: bfloat16 [6144, 256, 512], P(('row', 'col')), may hold values from -0.109375 to 0.109375
- tile_dst: int32 [6144], P(('row', 'col')), may hold values from 0 to 7
- tile_src: int32 [6144], P(('row', 'col')), may hold values from 0 to 127
- geometry: float32 [1024, 6, 256], P(('row', 'col')), may hold values from -5 to 5
- areas: float32 [1024, 256], P(('row', 'col')), may hold values from 0.25 to 2
- block_owner: int32 [1024, 1], P(('row', 'col')), may hold values from 0 to 7; in each aligned block of 8 rows (0 to 7, 8 to 15, ...) at most 2 rows name the same one
- block_slot: int32 [1024], P(('row', 'col')), may hold values from 0 to 3
Outputs:
- field: float32 [1024, 32, 256], P(('row', 'col'))
- shape_gradient: float32 [1024, 256], P(('row', 'col'))
Inputs may be any that keep to these rules, and one draw needn't show every extreme that they name: Among the blocks of one device at most 2 have the same block_owner, and some device reaches 2.
All inputs are finite; a program needn't handle non-finite values.
Results may differ from a plain program's by a relative error of at most 0.0003.
Values may be sent and summed in bfloat16 or wider, within the bound.
A program may use at most 64 MiB of HBM per device.

v0:
```python
import jax
import jax.numpy as jnp
from jax import lax
from jax.sharding import PartitionSpec as P

CAP = 2
PD = 4
EPSILON = 1e-05


def make_basis(geometry, areas):
    normal = geometry[:, 0:3]
    place = geometry[:, 3:6]
    twist = jnp.stack(
        [
            place[:, 1] * normal[:, 2] - place[:, 2] * normal[:, 1],
            place[:, 2] * normal[:, 0] - place[:, 0] * normal[:, 2],
            place[:, 0] * normal[:, 1] - place[:, 1] * normal[:, 0],
        ],
        axis=1,
    )
    weight = areas[:, None, :]
    return jnp.concatenate([weight * normal, weight * twist, weight, weight], axis=1)


def split_complex(images, freq_count, node_count):
    real_part = images[:, :freq_count, :node_count] - images[:, freq_count:, node_count:]
    imag_part = images[:, :freq_count, node_count:] + images[:, freq_count:, :node_count]
    return jnp.concatenate([real_part, imag_part], axis=1)


def normalize(totals):
    return totals * lax.rsqrt(jnp.mean(totals * totals, axis=1, keepdims=True) + EPSILON)


def shards(panels, tiles, tile_dst, tile_src, geometry, areas, block_owner, block_slot):
    precise = lax.Precision.HIGHEST
    block_count, rows_twice, node_count = panels.shape
    freq_count = rows_twice // 2
    tile_count = tiles.shape[0]
    flat_panels = panels.reshape(block_count, rows_twice * node_count)
    gathered = lax.all_gather(flat_panels, "row", axis=0, tiled=True)
    count = gathered.shape[0]
    picking = (tile_src[:, None] == jnp.arange(count, dtype=jnp.int32)[None, :]).astype(
        jnp.bfloat16
    )
    picked = jnp.dot(picking, gathered, preferred_element_type=jnp.float32)
    chosen = picked.astype(jnp.bfloat16).reshape(tile_count, rows_twice, node_count)
    images = jnp.einsum("tjn,tnm->tjm", chosen, tiles, preferred_element_type=jnp.float32)
    tile_terms = split_complex(images, freq_count, node_count)
    target = (tile_dst[None, :] == jnp.arange(block_count, dtype=jnp.int32)[:, None]).astype(
        jnp.float32
    )
    near = jnp.einsum("dt,tjn->djn", target, tile_terms, precision=precise)
    incident = panels.astype(jnp.float32)
    field = 0.5 * incident + near
    power = field[:, :freq_count] ** 2 + field[:, freq_count:] ** 2
    cross_power = (
        incident[:, :freq_count] * field[:, :freq_count]
        + incident[:, freq_count:] * field[:, freq_count:]
    )
    basis = make_basis(geometry, areas)
    first_moments = jnp.einsum("bkn,bfn->bkf", basis[:, :7], power, precision=precise)
    last_moment = jnp.einsum("bn,bfn->bf", basis[:, 7], cross_power, precision=precise)
    moments = jnp.concatenate([first_moments, last_moment[:, None, :]], axis=1).reshape(
        block_count, -1
    )
    moment_width = moments.shape[1]
    group_count = lax.axis_size("col")
    owner = block_owner[:, 0]
    block_index = jnp.arange(block_count, dtype=jnp.int32)
    same_owner = owner[:, None] == owner[None, :]
    earlier = block_index[None, :] < block_index[:, None]
    rank = jnp.sum(jnp.where(same_owner & earlier, 1, 0), axis=1)
    slot_target = owner * CAP + rank
    slot_index = jnp.arange(group_count * CAP, dtype=jnp.int32)
    placing = slot_index[:, None] == slot_target[None, :]
    place_float = placing.astype(jnp.float32)
    send_values = jnp.dot(place_float, moments, precision=precise).reshape(
        group_count, CAP, moment_width
    )
    send_labels = (
        jnp.sum(jnp.where(placing, block_slot[None, :] + 1, 0), axis=1).astype(jnp.float32) - 1.0
    ).reshape(group_count, CAP)
    received, labels = (
        lax.all_to_all(send_values, "col", split_axis=0, concat_axis=0, tiled=True),
        lax.all_to_all(send_labels, "col", split_axis=0, concat_axis=0, tiled=True),
    )
    member = (
        labels.reshape(-1)[None, :] == jnp.arange(PD, dtype=jnp.int32).astype(jnp.float32)[:, None]
    ).astype(jnp.float32)
    totals = jnp.dot(member, received.reshape(-1, moment_width), precision=precise)
    adjoint = normalize(totals)
    answer = jnp.dot(member.T, adjoint, precision=precise).reshape(group_count, CAP, moment_width)
    returned = lax.all_to_all(answer, "col", split_axis=0, concat_axis=0, tiled=True)
    block_adjoint = jnp.dot(place_float.T, returned.reshape(-1, moment_width), precision=precise)
    shaped = block_adjoint.reshape(block_count, 8, freq_count)
    first_terms = jnp.einsum("bkf,bfn->bkn", shaped[:, :7], power, precision=precise)
    last_term = jnp.einsum("bf,bfn->bn", shaped[:, 7], cross_power, precision=precise)
    shape_gradient = (
        jnp.sum(basis[:, :7] * first_terms, axis=1) + basis[:, 7] * last_term
    ) / freq_count
    return (field, shape_gradient)


def solution(mesh):
    in_specs = (
        P(("row", "col"), None, None),
        P(("row", "col"), None, None),
        P(("row", "col")),
        P(("row", "col")),
        P(("row", "col"), None, None),
        P(("row", "col"), None),
        P(("row", "col"), None),
        P(("row", "col")),
    )
    out_specs = (P(("row", "col"), None, None), P(("row", "col"), None))
    return jax.shard_map(shards, mesh=mesh, in_specs=in_specs, out_specs=out_specs, check_vma=False)
```

profile of v0, /device:TPU:0, one launch (start us, length us, event | category | flops | bytes accessed | tf_op | source)
XLA Modules:
  0.0 94.8 jit_solution(7106194001397986972)
XLA Ops:
  7.2 0.0 all-gather.2.cloned.1.call-start
  7.2 1.6 %copy.87 = bf16[1,8,32,256]{3,1,2,0:T(8,128)(2,1)} copy(bf16[1,8,32,256]{3,2,1,0:T(8,128)(2,1)} %bitcast.44) | data formatting | bytes 262144
  8.8 0.0 all-gather.2.cloned.1.call-update
  8.9 0.9 select_reduce_fusion.1
  9.8 0.7 multiply_add_fusion.2
  10.5 0.1 select_reduce_fusion
  10.6 0.7 sub.25
  11.2 7.0 %all-to-all-start = ((f32[8,1,2]{2,1,0:T(1,128)}), f32[8,1,2]{2,1,0:T(1,128)S(1)}, u32[]{:S(2)}, u32[]{:S(2)}) async-start(f32[8,1,2]{2,1,0:T(1,128)} %bitcast.3), calls=%async_computation | async-start | bytes 8192 | tf_op jit(solution)/shard_map/all_to_all | solution.py:87
  18.3 0.7 broadcast_in_dim.24
  19.0 0.7 slice.73
  19.7 0.8 fusion.42
  20.5 0.7 copy_multiply_fusion
  21.3 1.0 %copy_convert_fusion = f32[8,32,256]{2,0,1:T(8,128)S(1)} fusion(bf16[8,32,256]{2,1,0:T(8,128)(2,1)} %param.8), kind=kLoop, calls=%fused_computation.12 | loop fusion | flops 65536 | bytes 393216 | tf_op jit(solution)/shard_map/convert_element_type | solution.py:55
  22.3 24.3 %all-gather.2.cloned.1.call-done = bf16[128,8192]{1,0:T(8,128)(2,1)} async-done(((bf16[8,8192]{1,0:T(8,128)(2,1)}), bf16[128,8192]{1,0:T(8,128)(2,1)}) %all-gather.2.cloned.1.call-update) | async-done | bytes 2097168 | tf_op jit(solution)/shard_map/all_gather | solution.py:42
  46.6 2.1 %convolution_convert_fusion = bf16[48,8192]{1,0:T(8,128)(2,1)S(1)} fusion(bf16[128,8192]{1,0:T(8,128)(2,1)} %all-gather.2.cloned.1.call-done, s32[48]{0:T(128)} %param.11), kind=kOutput, calls=%fused_computation | convolution fusion | flops 101062656 | bytes 2883776 | tf_op jit(solution)/shard_map/dot_general | solution.py:47
  48.7 0.2 copy.88
  48.9 6.8 %fusion.43 = f32[48,32,512]{2,1,0:T(8,128)S(1)} fusion(bf16[48,32,256]{2,1,0:T(8,128)(2,1)S(1)} %bitcast.42, bf16[48,256,512]{2,1,0:T(8,128)(2,1)} %param.9), kind=kOutput, calls=%fused_computation.69 | convolution fusion | flops 402653184 | bytes 16515072 | tf_op jit(solution)/shard_map/tjn,tnm->tjm/dot_general | solution.py:49
  55.7 0.3 slice_subtract_fusion
  56.0 0.0 copy-start
  56.0 0.0 copy-start.2
  56.1 0.1 pad_maximum_fusion
  56.2 0.7 copy-done
  56.9 0.0 copy-done.2
  56.9 0.0 copy-start.1
  56.9 1.5 %fusion.2 = f32[8,32,256]{2,0,1:T(8,128)S(1)} fusion(f32[48,32,256]{2,1,0:T(8,128)S(1)} %pad_maximum_fusion, bf16[8,32,256]{2,1,0:T(8,128)(2,1)S(1)} %copy-done, s32[48]{0:T(128)S(1)} %copy-done.2), kind=kOutput, calls=%fused_computation.4 | convolution fusion | flops 37945728 | bytes 1966272 | tf_op jit(solution)/shard_map/dt,tjn->djn/dot_general | solution.py:54
  58.5 0.0 copy-done.1
  58.5 0.3 fusion.9
  58.8 0.3 fusion.12
  59.1 0.1 reshape.100
  59.2 0.2 fusion.19
  59.3 0.6 copy.70
  60.0 0.0 all-to-all-done
  60.0 6.6 %all-to-all-start.1 = ((f32[8,2,128]{2,1,0:T(2,128)}), f32[8,2,128]{2,1,0:T(2,128)S(1)}, u32[]{:S(2)}, u32[]{:S(2)}) async-start(f32[8,2,128]{2,1,0:T(2,128)} %copy.70), calls=%async_computation.1 | async-start | bytes 16384 | tf_op jit(solution)/shard_map/all_to_all | solution.py:86
  66.5 0.5 broadcast.78
  67.0 0.7 reduce.3
  67.7 0.1 eq.96
  67.8 6.4 %all-to-all-done.1 = f32[8,2,128]{2,1,0:T(2,128)S(1)} async-done(((f32[8,2,128]{2,1,0:T(2,128)}), f32[8,2,128]{2,1,0:T(2,128)S(1)}, u32[]{:S(2)}, u32[]{:S(2)}) %all-to-all-start.1) | async-done | bytes 8224 | tf_op jit(solution)/shard_map/all_to_all | solution.py:86
  74.2 0.3 multiply_reduce_fusion
  74.5 0.9 fusion.29
  75.4 3.3 %all-to-all-start.2 = ((f32[8,2,128]{2,1,0:T(2,128)}), f32[8,2,128]{2,1,0:T(2,128)S(1)}, u32[]{:S(2)}, u32[]{:S(2)}) async-start(f32[8,2,128]{2,1,0:T(2,128)} %bitcast.10), calls=%async_computation.2 | async-start | bytes 16384 | tf_op jit(solution)/shard_map/all_to_all | solution.py:95
  78.7 0.8 copy.74
  79.5 6.8 %all-to-all-done.2 = f32[8,2,128]{2,1,0:T(2,128)S(1)} async-done(((f32[8,2,128]{2,1,0:T(2,128)}), f32[8,2,128]{2,1,0:T(2,128)S(1)}, u32[]{:S(2)}, u32[]{:S(2)}) %all-to-all-start.2) | async-done | bytes 8224 | tf_op jit(solution)/shard_map/all_to_all | solution.py:95
  86.4 0.1 copy.71
  86.5 0.4 fusion.26
  86.8 0.3 fusion.5
  87.1 0.2 fusion.7
  87.4 0.6 fusion.17
  (9 shorter events, 0.1 us)
Async XLA Ops:
  7.2 39.5 %all-gather.2.cloned.1.call-start = ((), (), s32[]{:S(2)}) async-start(), calls=%async_computation.3 | async-start | bytes 2228224 | tf_op jit(solution)/shard_map/all_gather | solution.py:42
  11.2 48.7 %all-to-all-start = ((f32[8,1,2]{2,1,0:T(1,128)}), f32[8,1,2]{2,1,0:T(1,128)S(1)}, u32[]{:S(2)}, u32[]{:S(2)}) async-start(f32[8,1,2]{2,1,0:T(1,128)} %bitcast.3), calls=%async_computation | async-start | bytes 8192 | tf_op jit(solution)/shard_map/all_to_all | solution.py:87
  56.0 0.9 copy-start
  56.0 0.9 copy-start.2
  56.9 1.6 %copy-start.1 = (f32[8,256]{1,0:T(8,128)S(1)}, f32[8,256]{1,0:T(8,128)}, u32[]{:S(2)}) copy-start(f32[8,256]{1,0:T(8,128)} %param.13) | copy-start | bytes 24580
  60.0 14.3 %all-to-all-start.1 = ((f32[8,2,128]{2,1,0:T(2,128)}), f32[8,2,128]{2,1,0:T(2,128)S(1)}, u32[]{:S(2)}, u32[]{:S(2)}) async-start(f32[8,2,128]{2,1,0:T(2,128)} %copy.70), calls=%async_computation.1 | async-start | bytes 16384 | tf_op jit(solution)/shard_map/all_to_all | solution.py:86
  75.4 11.0 %all-to-all-start.2 = ((f32[8,2,128]{2,1,0:T(2,128)}), f32[8,2,128]{2,1,0:T(2,128)S(1)}, u32[]{:S(2)}, u32[]{:S(2)}) async-start(f32[8,2,128]{2,1,0:T(2,128)} %bitcast.10), calls=%async_computation.2 | async-start | bytes 16384 | tf_op jit(solution)/shard_map/all_to_all | solution.py:95
Sparse Core Ops, SparseCore 0:
  10.2 36.3 all-gather.1
where the time goes:
time: 95.4 us; the launch traced here: 94.8 us
  waiting for transfers between devices  37.6 us (39%)
  starting transfers between devices  17 us (18%)
  between operations  14.2 us (15%)
  matrix products  13.1 us (14%)
  local copies, waits for them, and re-layouts  7.64 us (8%)
  other arithmetic  5.25 us (6%)
    all_gather x1, waiting for transfers between devices, shards(): gathered = lax.all_gather(flat_panels, 'row', axis=0, tiled=True)  24.3 us
    all_to_all x1, starting transfers between devices, shards(): lax.all_to_all(send_labels, 'col', split_axis=0, concat_axis=0, tiled=True)  7.04 us
    all_to_all x1, waiting for transfers between devices, shards(): lax.all_to_all(answer, 'col', split_axis=0, concat_axis=0, tiled=True)  6.84 us
    dot_general x1, matrix products, shards(): jnp.einsum('tjn,tnm->tjm', chosen, tiles, preferred_element_type=jnp.floa...  6.83 us
    all_to_all x1, starting transfers between devices, shards(): lax.all_to_all(send_values, 'col', split_axis=0, concat_axis=0, tiled=True)  6.56 us
    all_to_all x1, waiting for transfers between devices, shards(): lax.all_to_all(send_values, 'col', split_axis=0, concat_axis=0, tiled=True)  6.43 us
    unnamed x9, local copies, waits for them, and re-layouts  3.35 us
    all_to_all x1, starting transfers between devices, shards(): lax.all_to_all(answer, 'col', split_axis=0, concat_axis=0, tiled=True)  3.33 us
  transfers between devices with their start and end apart: 4, of which 3 were waited for; matrix products, arithmetic and copies ran while one was open for 22% of the time, Pallas kernels for 0%

commit v1 on v0

--- a/solution.py
+++ b/solution.py
@@ -39,7 +39,9 @@
     freq_count = rows_twice // 2
     tile_count = tiles.shape[0]
     flat_panels = panels.reshape(block_count, rows_twice * node_count)
-    gathered = lax.all_gather(flat_panels, "row", axis=0, tiled=True)
+    gathered = jnp.concatenate(
+        lax.all_to_all(jnp.stack([flat_panels] * lax.axis_size("row")), "row", 0, 0), axis=0
+    )
     count = gathered.shape[0]
     picking = (tile_src[:, None] == jnp.arange(count, dtype=jnp.int32)[None, :]).astype(
         jnp.bfloat16

time: 95.4 us -> 84.8 us (0.89)
  between operations: 14.2 us -> 0.86 us
  starting transfers between devices: 17 us -> 23.9 us
  other arithmetic: 5.25 us -> 2.21 us
  waiting for transfers between devices: 37.6 us -> 39.9 us
  matrix products: 13.1 us -> 11.5 us
  local copies, waits for them, and re-layouts: 7.64 us -> 6.1 us
    all_to_all x0 -> x1, waiting for transfers between devices: none -> 26.6 us  [shards(): lax.all_to_all(jnp.stack([flat_panels] * lax.axis_size('row')), 'row', 0, 0)]
    all_gather x1 -> x0, waiting for transfers between devices: 24.3 us -> none  [shards(): gathered = lax.all_gather(flat_panels, 'row', axis=0, tiled=True)]
    all_to_all x0 -> x1, starting transfers between devices: none -> 6.69 us  [shards(): lax.all_to_all(jnp.stack([flat_panels] * lax.axis_size('row')), 'row', 0, 0)]
    dot_general x1, matrix products: 2.07 us -> 0.46 us  [shards(): picked = jnp.dot(picking, gathered, preferred_element_type=jnp.float32)]
    another operation x0 -> x1, local copies, waits for them, and re-layouts: none -> 1.54 us  [shards(): jnp.stack([flat_panels] * lax.axis_size('row'))]
    unnamed x9 -> x17, local copies, waits for them, and re-layouts: 3.35 us -> 2.48 us
  transfers between devices with their start and end apart: 4 -> 4, of which waited for: 3 -> 3; matrix products, arithmetic and copies ran while one was open for 22% -> 17% of each run, Pallas kernels for 0% -> 0%
where the time goes in v1:
time: 84.8 us; the launch traced here: 84.4 us
  waiting for transfers between devices  39.9 us (47%)
  starting transfers between devices  23.9 us (28%)
  matrix products  11.5 us (14%)
  local copies, waits for them, and re-layouts  6.1 us (7%)
  other arithmetic  2.21 us (3%)
  between operations  0.86 us (1%)
    all_to_all x1, waiting for transfers between devices, shards(): lax.all_to_all(jnp.stack([flat_panels] * lax.axis_size('row')), 'row', 0, 0)  26.6 us
    all_to_all x1, starting transfers between devices, shards(): lax.all_to_all(send_values, 'col', split_axis=0, concat_axis=0, tiled=True)  7.2 us
    all_to_all x1, waiting for transfers between devices, shards(): lax.all_to_all(answer, 'col', split_axis=0, concat_axis=0, tiled=True)  6.84 us
    dot_general x1, matrix products, shards(): jnp.einsum('tjn,tnm->tjm', chosen, tiles, preferred_element_type=jnp.floa...  6.83 us
    all_to_all x1, starting transfers between devices, shards(): lax.all_to_all(jnp.stack([flat_panels] * lax.axis_size('row')), 'row', 0, 0)  6.69 us
    all_to_all x1, starting transfers between devices, shards(): lax.all_to_all(send_labels, 'col', split_axis=0, concat_axis=0, tiled=True)  6.64 us
    all_to_all x1, waiting for transfers between devices, shards(): lax.all_to_all(send_values, 'col', split_axis=0, concat_axis=0, tiled=True)  6.43 us
    all_to_all x1, starting transfers between devices, shards(): lax.all_to_all(answer, 'col', split_axis=0, concat_axis=0, tiled=True)  3.33 us
  transfers between devices with their start and end apart: 4, of which 3 were waited for; matrix products, arithmetic and copies ran while one was open for 17% of the time, Pallas kernels for 0%

profile of v1, /device:TPU:0, one launch (start us, length us, event | category | flops | bytes accessed | tf_op | source)
XLA Modules:
  0.0 84.4 jit_solution(12633867401170301511)
XLA Ops:
  0.6 1.0 %copy.87 = bf16[1,8,32,256]{3,1,2,0:T(8,128)(2,1)S(1)} copy(bf16[1,8,32,256]{3,2,1,0:T(8,128)(2,1)} %bitcast.46) | data formatting | bytes 262144
  1.6 1.5 %stack.4 = bf16[16,8,8192]{2,1,0:T(8,128)(2,1)} broadcast(bf16[8,8192]{1,0:T(8,128)(2,1)S(1)} %bitcast.47), dimensions={1,2} | broadcast | bytes 2228224 | tf_op jit(solution)/shard_map/stack | solution.py:43
  3.2 0.0 slice-start
  3.2 0.0 copy-start
  3.2 0.0 copy-start.3
  3.2 6.7 %all-to-all-start = ((bf16[16,8,8192]{2,1,0:T(8,128)(2,1)}), bf16[16,8,8192]{2,1,0:T(8,128)(2,1)S(1)}, u32[]{:S(2)}, u32[]{:S(2)}) async-start(bf16[16,8,8192]{2,1,0:T(8,128)(2,1)} %stack.4), calls=%async_computation | async-start | bytes 4194304 | tf_op jit(solution)/shard_map/all_to_all | solution.py:43
  9.9 0.0 copy-done.1
  9.9 0.0 copy-done.5
  9.9 0.2 select_reduce_fusion.1
  10.1 0.0 copy-done.6
  10.1 0.1 select_reduce_fusion
  10.2 0.7 sub.25
  10.9 0.0 copy-done.2
  11.0 0.0 slice-done
  11.0 0.0 copy-done
  11.0 0.1 copy_convert_fusion
  11.1 26.6 %all-to-all-done = bf16[16,8,8192]{2,1,0:T(8,128)(2,1)S(1)} async-done(((bf16[16,8,8192]{2,1,0:T(8,128)(2,1)}), bf16[16,8,8192]{2,1,0:T(8,128)(2,1)S(1)}, u32[]{:S(2)}, u32[]{:S(2)}) %all-to-all-start) | async-done | bytes 2097184 | tf_op jit(solution)/shard_map/all_to_all | solution.py:43
  37.7 6.6 %all-to-all-start.1 = ((f32[8,1,2]{2,1,0:T(1,128)}), f32[8,1,2]{2,1,0:T(1,128)S(1)}, u32[]{:S(2)}, u32[]{:S(2)}) async-start(f32[8,1,2]{2,1,0:T(1,128)} %bitcast.4), calls=%async_computation.1 | async-start | bytes 8192 | tf_op jit(solution)/shard_map/all_to_all | solution.py:89
  44.3 0.0 copy-done.3
  44.4 0.5 convolution_convert_fusion
  44.8 0.2 copy.88
  45.0 6.8 %fusion.44 = f32[48,32,512]{2,1,0:T(8,128)S(1)} fusion(bf16[48,32,256]{2,1,0:T(8,128)(2,1)S(1)} %bitcast.44, bf16[48,256,512]{2,1,0:T(8,128)(2,1)} %param.9), kind=kOutput, calls=%fused_computation.70 | convolution fusion | flops 402653184 | bytes 16515072 | tf_op jit(solution)/shard_map/tjn,tnm->tjm/dot_general | solution.py:51
  51.8 0.3 slice_subtract_fusion
  52.1 0.0 copy-start.4
  52.2 0.1 pad_maximum_fusion
  52.3 0.5 copy-done.4
  52.8 1.5 %fusion.3 = f32[8,32,256]{2,0,1:T(8,128)S(1)} fusion(f32[48,32,256]{2,1,0:T(8,128)S(1)} %pad_maximum_fusion, bf16[8,32,256]{2,1,0:T(8,128)(2,1)S(1)} %copy-done, s32[48]{0:T(128)S(1)} %copy-done.4), kind=kOutput, calls=%fused_computation.5 | convolution fusion | flops 37945728 | bytes 1966272 | tf_op jit(solution)/shard_map/dt,tjn->djn/dot_general | solution.py:56
  54.3 0.3 fusion.10
  54.6 0.3 fusion.13
  54.9 0.1 reshape.102
  55.0 0.2 fusion.20
  55.2 0.6 copy.70
  55.8 0.0 all-to-all-done.1
  55.8 7.2 %all-to-all-start.2 = ((f32[8,2,128]{2,1,0:T(2,128)}), f32[8,2,128]{2,1,0:T(2,128)S(1)}, u32[]{:S(2)}, u32[]{:S(2)}) async-start(f32[8,2,128]{2,1,0:T(2,128)} %copy.70), calls=%async_computation.2 | async-start | bytes 16384 | tf_op jit(solution)/shard_map/all_to_all | solution.py:88
  63.0 0.5 broadcast.79
  63.5 0.7 reduce.3
  64.2 0.1 eq.96
  64.3 6.4 %all-to-all-done.2 = f32[8,2,128]{2,1,0:T(2,128)S(1)} async-done(((f32[8,2,128]{2,1,0:T(2,128)}), f32[8,2,128]{2,1,0:T(2,128)S(1)}, u32[]{:S(2)}, u32[]{:S(2)}) %all-to-all-start.2) | async-done | bytes 8224 | tf_op jit(solution)/shard_map/all_to_all | solution.py:88
  70.7 0.3 multiply_reduce_fusion
  71.0 0.9 %fusion.30 = f32[16,128]{1,0:T(8,128)} fusion(f32[4,128]{1,0:T(4,128)S(1)} %get-tuple-element.26, f32[4]{0:T(128)S(1)} %add_rsqrt_fusion, f32[16]{0:T(128)S(1)} %eq.96, f32[4]{0:T(128)S(1)} %iota_convert_fusion), kind=kOutput, calls=%fused_computation.49 | convolution fusion | flops 98880 | bytes 10336 | tf_op jit(solution)/shard_map/dot_general | solution.py:96
  71.9 3.3 %all-to-all-start.3 = ((f32[8,2,128]{2,1,0:T(2,128)}), f32[8,2,128]{2,1,0:T(2,128)S(1)}, u32[]{:S(2)}, u32[]{:S(2)}) async-start(f32[8,2,128]{2,1,0:T(2,128)} %bitcast.11), calls=%async_computation.3 | async-start | bytes 16384 | tf_op jit(solution)/shard_map/all_to_all | solution.py:97
  75.2 0.8 copy.74
  76.0 6.8 %all-to-all-done.3 = f32[8,2,128]{2,1,0:T(2,128)S(1)} async-done(((f32[8,2,128]{2,1,0:T(2,128)}), f32[8,2,128]{2,1,0:T(2,128)S(1)}, u32[]{:S(2)}, u32[]{:S(2)}) %all-to-all-start.3) | async-done | bytes 8224 | tf_op jit(solution)/shard_map/all_to_all | solution.py:97
  82.9 0.1 copy.71
  83.0 0.4 fusion.27
  83.3 0.3 fusion.6
  83.6 0.2 fusion.8
  83.8 0.6 fusion.18
  (17 shorter events, 0.2 us)
Async XLA Ops:
  3.2 6.7 %copy-start.1 = (f32[8,256]{1,0:T(8,128)S(1)}, f32[8,256]{1,0:T(8,128)}, u32[]{:S(2)}) copy-start(f32[8,256]{1,0:T(8,128)} %param.13) | copy-start | bytes 24580
  3.2 6.8 %copy-start.5 = (s32[8,1]{0,1:T(1,128)S(1)}, s32[8,1]{0,1:T(1,128)}, u32[]{:S(2)}) copy-start(s32[8,1]{0,1:T(1,128)} %param.14) | copy-start | bytes 100
  3.2 7.0 %copy-start.6 = (s32[8]{0:T(128)S(1)}, s32[8]{0:T(128)}, u32[]{:S(2)}) copy-start(s32[8]{0:T(128)} %param.15) | copy-start | bytes 100
  3.2 7.7 %copy-start.2 = (f32[8,6,256]{2,0,1:T(8,128)S(1)}, f32[8,6,256]{2,0,1:T(8,128)}, u32[]{:S(2)}) copy-start(f32[8,6,256]{2,0,1:T(8,128)} %param.12) | copy-start | bytes 147460
  3.2 7.8 %slice-start = ((f32[8,6,256]{2,0,1:T(8,128)}), f32[8,3,256]{2,0,1:T(8,128)S(1)}, s32[]{:S(2)}) async-start(f32[8,6,256]{2,0,1:T(8,128)} %param.12), calls=%async_computation.4 | async-start | bytes 49152 | tf_op jit(solution)/shard_map/slice | solution.py:12
  3.2 7.9 %copy-start = (bf16[8,32,256]{2,1,0:T(8,128)(2,1)S(1)}, bf16[8,32,256]{2,1,0:T(8,128)(2,1)}, u32[]{:S(2)}) copy-start(bf16[8,32,256]{2,1,0:T(8,128)(2,1)} %param.8) | copy-start | bytes 393220
  3.2 41.2 %copy-start.3 = (s32[48]{0:T(128)S(1)}, s32[48]{0:T(128)}, u32[]{:S(2)}) copy-start(s32[48]{0:T(128)} %param.11) | copy-start | bytes 580
  3.2 34.5 %all-to-all-start = ((bf16[16,8,8192]{2,1,0:T(8,128)(2,1)}), bf16[16,8,8192]{2,1,0:T(8,128)(2,1)S(1)}, u32[]{:S(2)}, u32[]{:S(2)}) async-start(bf16[16,8,8192]{2,1,0:T(8,128)(2,1)} %stack.4), calls=%async_computation | async-start | bytes 4194304 | tf_op jit(solution)/shard_map/all_to_all | solution.py:43
  37.7 18.1 %all-to-all-start.1 = ((f32[8,1,2]{2,1,0:T(1,128)}), f32[8,1,2]{2,1,0:T(1,128)S(1)}, u32[]{:S(2)}, u32[]{:S(2)}) async-start(f32[8,1,2]{2,1,0:T(1,128)} %bitcast.4), calls=%async_computation.1 | async-start | bytes 8192 | tf_op jit(solution)/shard_map/all_to_all | solution.py:89
  52.1 0.7 copy-start.4
  55.8 14.9 %all-to-all-start.2 = ((f32[8,2,128]{2,1,0:T(2,128)}), f32[8,2,128]{2,1,0:T(2,128)S(1)}, u32[]{:S(2)}, u32[]{:S(2)}) async-start(f32[8,2,128]{2,1,0:T(2,128)} %copy.70), calls=%async_computation.2 | async-start | bytes 16384 | tf_op jit(solution)/shard_map/all_to_all | solution.py:88
  71.9 11.0 %all-to-all-start.3 = ((f32[8,2,128]{2,1,0:T(2,128)}), f32[8,2,128]{2,1,0:T(2,128)S(1)}, u32[]{:S(2)}, u32[]{:S(2)}) async-start(f32[8,2,128]{2,1,0:T(2,128)} %bitcast.11), calls=%async_computation.3 | async-start | bytes 16384 | tf_op jit(solution)/shard_map/all_to_all | solution.py:97
